TPU v7x, 32 devices: a whole 2x2x4 slice. The times are simulated.
32 devices in a mesh: blen: 4 (over z), tm: 8 (over y, x, core).
Axes of the slice: x: 2, y: 2, z: 4, core: 2. Of those that a mesh axis runs over, the one named last changes fastest.
Arguments:
- model_grid: bfloat16 [256, 2, 512, 512], P(('blen', 'tm')), may hold values from -6 to 6
- vis_values: float32 [2, 16384], P(None, ('blen', 'tm')), may hold values from -6 to 6
- weights: float32 [16384], P(('blen', 'tm')), may hold values from 0.3 to 3
- flags: int32 [16384], P(('blen', 'tm')), may hold values 0 or 1
- uv_frac: float32 [2, 16384], P(None, ('blen', 'tm')), may hold values from 0 to 1
- cell_offset: int32 [2, 16384], P(None, ('blen', 'tm')), may hold values from 3 to 507
- tile_index: int32 [16384, 1], P(('blen', 'tm')), may hold values from 0 to 255; in each aligned block of 512 rows (0 to 511, 512 to 1023, ...) at most 4 rows name the same one
Outputs:
- gradient: float32 [8192, 8192], P(('blen', 'tm'))
- weighted_residual: float32 [2, 16384], P(None, ('blen', 'tm'))
Inputs may be any that keep to these rules, and one draw needn't show every extreme that they name: `tile_index`: in the rows of one device no tile is named by more than 4 rows, and some device has a tile named by exactly 4 rows.
All inputs are finite; a program needn't handle non-finite values. No bound on the sum of `flags` on one device may be relied on, other than what follows from the above.
Results may differ from a plain program's by a relative error of at most 0.0095.
Values sent between devices are 32-bit elements; how exact they have to be, the bound alone decides.
No kernel may reach another device: no remote copies, remote signals or barrier semaphores. Data moves between devices by JAX's collectives and lax.ppermute only.
A program may use at most 192 MiB of HBM per device.

v0:
```python
import math
import jax
import jax.numpy as jnp
from jax import lax
from jax.sharding import PartitionSpec as P

NPIX = 8192
KSUP = 8
NT = 16
MOST = 4
kernel_scale = 0.5
highest = lax.Precision.HIGHEST


def taps_full(offsets, fractions, tile_side):
    cell_ids = lax.broadcasted_iota(jnp.int32, offsets.shape + (tile_side,), offsets.ndim)
    shifted = cell_ids - offsets[..., None]
    distance = shifted.astype(jnp.float32) - fractions[..., None]
    inside = (shifted >= 1 - KSUP // 2) & (shifted <= KSUP // 2)
    values = jnp.exp(-kernel_scale * distance * distance)
    return jnp.where(inside, values, 0.0).astype(jnp.bfloat16)


def phase_table(row_count, col_count, period):
    row_ids = lax.broadcasted_iota(jnp.int32, (row_count, col_count), 0)
    col_ids = lax.broadcasted_iota(jnp.int32, (row_count, col_count), 1)
    angles = 2.0 * math.pi / period * (row_ids * col_ids % period).astype(jnp.float32)
    return (jnp.cos(angles), jnp.sin(angles))


def complex_block(cos_part, sin_part):
    return jnp.stack([jnp.stack([cos_part, -sin_part]), jnp.stack([sin_part, cos_part])])


def on_device(model_grid, vis_values, weights, flags, uv_frac, cell_offset, tile_index):
    blen_size = lax.axis_size("blen")
    tm_size = lax.axis_size("tm")
    devices = blen_size * tm_size
    per_dev = model_grid.shape[0]
    tile_side = model_grid.shape[2]
    vis_count = weights.shape[0]
    ntiles = per_dev * devices
    total_slots = ntiles * MOST
    tile_ids = tile_index[:, 0]
    matches = tile_ids[:, None] == lax.broadcasted_iota(jnp.int32, (vis_count, ntiles), 1)
    counts = jnp.sum(matches.astype(jnp.int32), axis=0)
    starts = jnp.cumsum(counts) - counts
    sorting = jnp.argsort(tile_ids, stable=True)
    position = (
        jnp.zeros((vis_count,), jnp.int32).at[sorting].set(jnp.arange(vis_count, dtype=jnp.int32))
    )
    first_slot = jnp.sum(jnp.where(matches, starts[None, :], 0), axis=1)
    rank_in_tile = position - first_slot
    owner_dev = tile_ids // per_dev
    local_tile = tile_ids % per_dev
    slot_of = (local_tile * devices + owner_dev) * MOST + rank_in_tile
    weighted = weights * flags.astype(jnp.float32)
    float_fields = jnp.stack([vis_values[0], vis_values[1], weighted, uv_frac[0], uv_frac[1]])
    send_float = jnp.zeros((5, total_slots), jnp.float32).at[:, slot_of].set(float_fields)
    send_int = jnp.zeros((2, total_slots), jnp.int32).at[:, slot_of].set(cell_offset)
    recv_float, recv_int = (
        lax.all_to_all(
            send_float.reshape(5, per_dev, devices, MOST),
            ("blen", "tm"),
            split_axis=2,
            concat_axis=2,
            tiled=True,
        ),
        lax.all_to_all(
            send_int.reshape(2, per_dev, devices, MOST),
            ("blen", "tm"),
            split_axis=2,
            concat_axis=2,
            tiled=True,
        ),
    )
    owner_rows = devices * MOST
    block_rows = 512 if owner_rows % 512 == 0 else owner_rows
    block_count = owner_rows // block_rows
    float_blocks = recv_float.reshape(5, per_dev, block_count, block_rows).transpose(2, 0, 1, 3)
    int_blocks = recv_int.reshape(2, per_dev, block_count, block_rows).transpose(2, 0, 1, 3)

    def grid_step(adjoint, inputs):
        part_float, part_int = inputs
        taps_u = taps_full(part_int[0], part_float[3], tile_side)
        taps_v = taps_full(part_int[1], part_float[4], tile_side)
        partial_sums = jnp.einsum(
            "qrj,qcji->qrci", taps_v, model_grid, preferred_element_type=jnp.float32
        )
        predicted = jnp.sum(partial_sums * taps_u[:, :, None, :], axis=-1)
        observed = jnp.stack([part_float[0], part_float[1]], axis=-1)
        residual = part_float[2][..., None] * (predicted - observed)
        spread = (residual[..., None] * taps_u[:, :, None, :]).astype(jnp.bfloat16)
        adjoint = adjoint + jnp.einsum(
            "qrj,qrci->qcji", taps_v, spread, preferred_element_type=jnp.float32
        )
        return (adjoint, jnp.moveaxis(residual, -1, 0))

    start_adjoint = jnp.zeros((per_dev, 2, tile_side, tile_side), jnp.float32)
    adjoint, residual_blocks = lax.scan(grid_step, start_adjoint, (float_blocks, int_blocks))
    residual_slots = residual_blocks.transpose(1, 2, 0, 3).reshape(2, per_dev, owner_rows)
    returned = lax.all_to_all(
        residual_slots.reshape(2, per_dev, devices, MOST),
        ("blen", "tm"),
        split_axis=2,
        concat_axis=2,
        tiled=True,
    )
    weighted_residual = returned.reshape(2, total_slots)[:, slot_of]
    relaid = lax.all_to_all(adjoint, "tm", split_axis=2, concat_axis=0, tiled=True)
    tile_cols = NT // blen_size
    col_slice = tile_side // tm_size
    pieces = relaid.reshape(NT, tile_cols, 2, col_slice, tile_side)
    cos_small, sin_small = phase_table(NT, NT, NT)
    small_turn = complex_block(cos_small, sin_small)
    cos_twist, sin_twist = phase_table(NT, tile_side, NPIX)
    cos_tile, sin_tile = phase_table(tile_side, tile_side, tile_side)
    tile_turn = complex_block(cos_tile, sin_tile)
    section_one = jnp.einsum("acnt,tvcji->anvji", small_turn, pieces, precision=highest)
    twist_c = cos_twist[:, None, None, :]
    twist_s = sin_twist[:, None, None, :]
    turned = jnp.stack(
        [
            section_one[0] * twist_c - section_one[1] * twist_s,
            section_one[0] * twist_s + section_one[1] * twist_c,
        ]
    )
    columns = jnp.einsum("acmi,cnvji->amnvj", tile_turn, turned, precision=highest)
    rows_dev = NPIX // devices
    spread_cols = rows_dev * tile_cols * col_slice
    packed = columns.reshape(2, 1, devices, spread_cols)
    landed = lax.all_to_all(packed, ("blen", "tm"), split_axis=2, concat_axis=1, tiled=True)
    landed = landed.reshape(2, blen_size, tm_size, rows_dev, tile_cols, col_slice)
    small_split = small_turn.reshape(2, 2, NT, blen_size, tile_cols)
    section_two = jnp.einsum("acnpv,cptrvj->antrj", small_split, landed, precision=highest)
    twist_cv = cos_twist.reshape(NT, tm_size, 1, col_slice)
    twist_sv = sin_twist.reshape(NT, tm_size, 1, col_slice)
    turned_rows = jnp.stack(
        [
            section_two[0] * twist_cv - section_two[1] * twist_sv,
            section_two[0] * twist_sv + section_two[1] * twist_cv,
        ]
    )
    real_turn = jnp.stack([cos_tile, -sin_tile]).reshape(2, tile_side, tm_size, col_slice)
    image_rows = jnp.einsum("cmtj,cntrj->rmn", real_turn, turned_rows, precision=highest)
    gradient = image_rows.reshape(rows_dev, NPIX) / NPIX
    return (gradient, weighted_residual)


def solution(mesh):
    in_specs = (
        P(("blen", "tm"), None, None, None),
        P(None, ("blen", "tm")),
        P(("blen", "tm")),
        P(("blen", "tm")),
        P(None, ("blen", "tm")),
        P(None, ("blen", "tm")),
        P(("blen", "tm"), None),
    )
    out_specs = (P(("blen", "tm"), None), P(None, ("blen", "tm")))
    return jax.shard_map(
        on_device, mesh=mesh, in_specs=in_specs, out_specs=out_specs, check_vma=False
    )
```

profile of v0, /device:TPU:0, one launch (start us, length us, event | category | flops | bytes accessed | tf_op | source)
XLA Modules:
  0.0 1047.1 jit_solution(14593329809357333968)
XLA Ops:
  14.8 7.3 all-to-all-start.1
  33.3 7.1 all-to-all-done
  43.2 5.3 multiply_reduce_fusion
  48.5 7.2 convolution_bitcast_fusion
  55.7 25.1 %copy.78 = f32[8,2,512,512]{3,1,0,2:T(2,128)} copy(f32[8,2,512,512]{2,3,1,0:T(8,128)} %convolution_bitcast_fusion) | data formatting | bytes 33554432 | tf_op jit(solution)/shard_map/while/body/eval_jaxpr/qrj,qrci->qcji/transpose | solution.py:94
  80.8 6.0 all-to-all-start.2
  97.8 173.0 %all-to-all-done.2 = f32[8,2,512,512]{3,1,0,2:T(2,128)} async-done(((f32[8,2,512,512]{3,1,0,2:T(2,128)}), f32[8,2,512,512]{3,1,0,2:T(2,128)}, u32[]{:S(2)}, u32[]{:S(2)}) %all-to-all-start.2) | async-done | bytes 16777248 | tf_op jit(solution)/shard_map/all_to_all | solution.py:110
  273.4 11.0 %copy.79 = f32[8,2,512,512]{3,2,1,0:T(8,128)S(1)} copy(f32[8,2,512,512]{3,1,0,2:T(2,128)} %all-to-all-done.2) | data formatting | bytes 33554432 | tf_op jit(solution)/shard_map/all_to_all | solution.py:110
  284.4 6.7 copy.80
  291.1 42.0 %fusion.11 = f32[2,16,4,64,512]{4,1,3,2,0:T(8,128)} fusion(f32[16,4,2,64,512]{4,3,2,1,0:T(8,128)} %bitcast.109, f32[1,2,16,16]{3,2,1,0:T(8,128)S(1)} %get-tuple-element.44, f32[1,2,16,16]{3,2,1,0:T(8,128)S(1)} %get-tuple-element.43), kind=kOutput, calls=%fused_computation.23 | convolution fusion | flops 1610613760 | bytes 33558528 | tf_op jit(solution)/shard_map/acnt,tvcji->anvji/dot_general | solution.py:119
  333.1 7.1 multiply_subtract_fusion.1
  340.2 6.4 pad_maximum_fusion
  346.6 67.2 %fusion.14 = f32[2,512,16,4,64]{1,4,3,2,0:T(8,128)} fusion(f32[2,16,4,64,512]{4,1,3,2,0:T(8,128)} %pad_maximum_fusion, f32[1,2,512,512]{3,2,1,0:T(8,128)S(1)} %copy-done, f32[1,2,512,512]{3,2,1,0:T(8,128)S(1)} %get-tuple-element.34), kind=kOutput, calls=%fused_computation.24 | convolution fusion | flops 51540656128 | bytes 37748736 | tf_op jit(solution)/shard_map/acmi,cnvji->amnvj/dot_general | solution.py:128
  413.8 31.1 %copy.83 = f32[2,512,16,4,64]{4,3,2,1,0:T(4,128)} copy(f32[2,512,16,4,64]{1,4,3,2,0:T(8,128)} %fusion.14) | data formatting | bytes 33554432 | tf_op jit(solution)/shard_map/acmi,cnvji->amnvj/dot_general | solution.py:128
  444.9 27.4 %reshape.436 = f32[2,1,32,65536]{3,2,0,1:T(8,128)} reshape(f32[2,512,16,4,64]{4,3,2,1,0:T(4,128)} %copy.83) | data formatting | bytes 33554432 | tf_op jit(solution)/shard_map/reshape | solution.py:131
  472.2 28.6 %copy.84 = f32[2,1,32,65536]{3,0,1,2:T(2,128)} copy(f32[2,1,32,65536]{3,2,0,1:T(8,128)} %reshape.436) | data formatting | bytes 33554432 | tf_op jit(solution)/shard_map/reshape | solution.py:131
  500.9 6.0 all-to-all-start.3
  516.5 363.0 %all-to-all-done.3 = f32[2,1,32,65536]{3,0,1,2:T(2,128)} async-done(((f32[2,1,32,65536]{3,0,1,2:T(2,128)}), f32[2,1,32,65536]{3,0,1,2:T(2,128)}, u32[]{:S(2)}, u32[]{:S(2)}) %all-to-all-start.3) | async-done | bytes 16777248 | tf_op jit(solution)/shard_map/all_to_all | solution.py:132
  879.5 38.4 %reshape.487 = f32[2,4,8,256,4,64]{5,4,3,0,2,1:T(4,128)} reshape(f32[2,1,32,65536]{3,0,1,2:T(2,128)} %all-to-all-done.3) | data formatting | bytes 33554432 | tf_op jit(solution)/shard_map/reshape | solution.py:133
  918.0 30.9 %copy.86 = f32[2,4,8,256,4,64]{3,4,1,0,5,2:T(4,128)} copy(f32[2,4,8,256,4,64]{5,4,3,0,2,1:T(4,128)} %reshape.487) | data formatting | bytes 33554432 | tf_op jit(solution)/shard_map/reshape | solution.py:133
  948.8 31.8 %fusion.17 = f32[2,16,8,256,64]{3,1,4,2,0:T(8,128)S(1)} fusion(f32[2,4,8,256,4,64]{3,4,1,0,5,2:T(4,128)} %copy.86, f32[2,2,16,4,4,1,1]{2,4,3,1,6,5,0:T(4,128)S(1)} %maximum_bitcast_fusion.17), kind=kOutput, calls=%fused_computation.25 | convolution fusion | flops 1610612736 | bytes 33558528 | tf_op jit(solution)/shard_map/acnpv,cptrvj->antrj/dot_general | solution.py:135
  985.2 42.3 %fusion.10 = f32[256,512,16]{1,0,2:T(8,128)} fusion(f32[2,16,8,256,64]{3,1,4,2,0:T(8,128)S(1)} %pad_maximum_fusion.1, f32[1,512,8,64]{1,3,2,0:T(8,128)S(1)} %get-tuple-element.56, f32[1,512,8,64]{1,3,2,0:T(8,128)S(1)} %get-tuple-element.57), kind=kOutput, calls=%fused_computation.18 | convolution fusion | flops 25772425216 | bytes 27262976 | tf_op jit(solution)/shard_map/cmtj,cntrj->rmn/dot_general | solution.py:145
  1027.6 10.3 copy.88
  1037.9 8.9 copy.92
  (68 shorter events, 55.8 us)
Async XLA Ops:
  11.4 14.1 %copy-start.1 = (s32[512]{0:T(512)}, s32[512]{0:T(512)S(1)}, u32[]{:S(2)}) copy-start(s32[512]{0:T(512)S(1)} %compare_select_fusion) | copy-start | bytes 6148
  14.8 15.5 %all-to-all-start.1 = ((s32[2,8,32,4]{1,3,0,2:T(4,128)}), s32[2,8,32,4]{1,3,0,2:T(4,128)S(1)}, u32[]{:S(2)}, u32[]{:S(2)}) async-start(s32[2,8,32,4]{1,3,0,2:T(4,128)} %copy.70), calls=%async_computation.1 | async-start | bytes 262144 | tf_op jit(solution)/shard_map/all_to_all | solution.py:69
  30.3 10.1 all-to-all-start
  80.8 190.0 %all-to-all-start.2 = ((f32[8,2,512,512]{3,1,0,2:T(2,128)}), f32[8,2,512,512]{3,1,0,2:T(2,128)}, u32[]{:S(2)}, u32[]{:S(2)}) async-start(f32[8,2,512,512]{3,1,0,2:T(2,128)} %copy.78), calls=%async_computation.2 | async-start | bytes 33554432 | tf_op jit(solution)/shard_map/all_to_all | solution.py:110
  270.8 230.0 %all-to-all-start.4 = ((f32[2,8,32,4]{1,3,0,2:T(4,128)}), f32[2,8,32,4]{1,3,0,2:T(4,128)S(1)}, u32[]{:S(2)}, u32[]{:S(2)}) async-start(f32[2,8,32,4]{1,3,0,2:T(4,128)} %copy.90), calls=%async_computation.4 | async-start | bytes 262144 | tf_op jit(solution)/shard_map/all_to_all | solution.py:102
  340.2 6.4 copy-start
  500.9 6.0 copy-start.2
  500.9 378.7 %all-to-all-start.3 = ((f32[2,1,32,65536]{3,0,1,2:T(2,128)}), f32[2,1,32,65536]{3,0,1,2:T(2,128)}, u32[]{:S(2)}, u32[]{:S(2)}) async-start(f32[2,1,32,65536]{3,0,1,2:T(2,128)} %copy.84), calls=%async_computation.3 | async-start | bytes 33554432 | tf_op jit(solution)/shard_map/all_to_all | solution.py:132
where the time goes:
time: 1060 us; the launch traced here: 1050 us
  waiting for transfers between devices  546 us (52%)
  local copies, waits for them, and re-layouts  235 us (22%)
  matrix products  196 us (18%)
  other arithmetic  44 us (4%)
  starting transfers between devices  24.7 us (2%)
    all_to_all x1, waiting for transfers between devices, on_device(): lax.all_to_all(packed, ('blen', 'tm'), split_axis=2, concat_axis=1, tiled...  363 us
    all_to_all x1, waiting for transfers between devices, on_device(): lax.all_to_all(adjoint, 'tm', split_axis=2, concat_axis=0, tiled=True)  173 us
    reshape x2, local copies, waits for them, and re-layouts, on_device(): landed.reshape(2, blen_size, tm_size, rows_dev, tile_cols, col_slice)  69.3 us
    dot_general x1, matrix products, on_device(): jnp.einsum('acmi,cnvji->amnvj', tile_turn, turned, precision=highest)  67.2 us
    reshape x2, local copies, waits for them, and re-layouts, on_device(): packed = columns.reshape(2, 1, devices, spread_cols)  56 us
    dot_general x1, matrix products, on_device(): jnp.einsum('cmtj,cntrj->rmn', real_turn, turned_rows, precision=highest)  42.3 us
    dot_general x1, matrix products, on_device(): jnp.einsum('acnt,tvcji->anvji', small_turn, pieces, precision=highest)  42 us
    dot_general x1, matrix products, on_device(): jnp.einsum('acnpv,cptrvj->antrj', small_split, landed, precision=highest)  31.8 us
  transfers between devices with their start and end apart: 5, of which 4 were waited for; matrix products, arithmetic and copies ran while one was open for 24% of the time, Pallas kernels for 0%

commit v1 on v0

--- a/solution.py
+++ b/solution.py
@@ -10,6 +10,17 @@
 MOST = 4
 kernel_scale = 0.5
 highest = lax.Precision.HIGHEST
+
+
+def split_up(x, dim, size):
+    before, after = (x.shape[:dim], x.shape[dim + 1 :])
+    return jnp.moveaxis(x.reshape(*before, size, -1, *after), dim, 0)
+
+
+def joined_along(blocks, dim):
+    blocks = jnp.moveaxis(blocks, 0, dim)
+    shape = blocks.shape
+    return blocks.reshape(*shape[:dim], shape[dim] * shape[dim + 1], *shape[dim + 2 :])
 
 
 def taps_full(offsets, fractions, tile_side):
@@ -107,7 +118,15 @@
         tiled=True,
     )
     weighted_residual = returned.reshape(2, total_slots)[:, slot_of]
-    relaid = lax.all_to_all(adjoint, "tm", split_axis=2, concat_axis=0, tiled=True)
+    size, index = (lax.axis_size("tm"), lax.axis_index("tm"))
+    parts = split_up(adjoint, 2, size)
+    out = parts
+    for step in range(1, size):
+        target, source = ((index + step) % size, (index - step) % size)
+        sent = lax.dynamic_index_in_dim(parts, target, 0)
+        partner_block = lax.ppermute(sent, "tm", [(i, (i + step) % size) for i in range(size)])
+        out = lax.dynamic_update_slice_in_dim(out, partner_block, source, axis=0)
+    relaid = joined_along(out, 0)
     tile_cols = NT // blen_size
     col_slice = tile_side // tm_size
     pieces = relaid.reshape(NT, tile_cols, 2, col_slice, tile_side)

time: 1060 us -> 1020 us (0.962)
  waiting for transfers between devices: 546 us -> 470 us
  starting transfers between devices: 24.7 us -> 65.4 us
    all_to_all x1 -> x0, waiting for transfers between devices: 173 us -> none  [on_device(): lax.all_to_all(adjoint, 'tm', split_axis=2, concat_axis=0, tiled=True)]
    ppermute x0 -> x7, waiting for transfers between devices: none -> 97.5 us  [on_device(): lax.ppermute(sent, 'tm', [(i, (i + step) % size) for i in range(size)])]
    ppermute x0 -> x7, starting transfers between devices: none -> 46.6 us  [on_device(): lax.ppermute(sent, 'tm', [(i, (i + step) % size) for i in range(size)])]
    transpose x1 -> x0, local copies, waits for them, and re-layouts: 25.1 us -> none  [grid_step(): jnp.einsum('qrj,qrci->qcji', taps_v, spread, preferred_element_type=jnp.f...]
    dynamic_update_slice x0 -> x7, local copies, waits for them, and re-layouts: none -> 20.7 us  [on_device(): out = lax.dynamic_update_slice_in_dim(out, partner_block, source, axis=0)]
    all_to_all x2 -> x0, local copies, waits for them, and re-layouts: 17.7 us -> none  [on_device(): lax.all_to_all(adjoint, 'tm', split_axis=2, concat_axis=0, tiled=True)]
    reshape x0 -> x1, local copies, waits for them, and re-layouts: none -> 12 us  [split_up(): return jnp.moveaxis(x.reshape(*before, size, -1, *after), dim, 0)]
    dynamic_slice x0 -> x1, local copies, waits for them, and re-layouts: none -> 11.1 us  [on_device(): sent = lax.dynamic_index_in_dim(parts, target, 0)]
  transfers between devices with their start and end apart: 5 -> 11, of which waited for: 4 -> 7; matrix products, arithmetic and copies ran while one was open for 24% -> 26% of each run, Pallas kernels for 0% -> 0%
where the time goes in v1:
time: 1020 us; the launch traced here: 1010 us
  waiting for transfers between devices  470 us (46%)
  local copies, waits for them, and re-layouts  239 us (23%)
  matrix products  187 us (18%)
  starting transfers between devices  65.4 us (6%)
  other arithmetic  46.2 us (5%)
    all_to_all x1, waiting for transfers between devices, on_device(): lax.all_to_all(packed, ('blen', 'tm'), split_axis=2, concat_axis=1, tiled...  362 us
    ppermute x7, waiting for transfers between devices, on_device(): lax.ppermute(sent, 'tm', [(i, (i + step) % size) for i in range(size)])  97.5 us
    reshape x2, local copies, waits for them, and re-layouts, on_device(): landed.reshape(2, blen_size, tm_size, rows_dev, tile_cols, col_slice)  69.3 us
    dot_general x1, matrix products, on_device(): jnp.einsum('acmi,cnvji->amnvj', tile_turn, turned, precision=highest)  67 us
    reshape x2, local copies, waits for them, and re-layouts, on_device(): packed = columns.reshape(2, 1, devices, spread_cols)  55.8 us
    ppermute x7, starting transfers between devices, on_device(): lax.ppermute(sent, 'tm', [(i, (i + step) % size) for i in range(size)])  46.6 us
    dot_general x1, matrix products, on_device(): jnp.einsum('cmtj,cntrj->rmn', real_turn, turned_rows, precision=highest)  42.3 us
    dot_general x1, matrix products, on_device(): jnp.einsum('acnt,tvcji->anvji', small_turn, pieces, precision=highest)  33.1 us
  transfers between devices with their start and end apart: 11, of which 7 were waited for; matrix products, arithmetic and copies ran while one was open for 26% of the time, Pallas kernels for 0%

profile of v1, /device:TPU:0, one launch (start us, length us, event | category | flops | bytes accessed | tf_op | source)
XLA Modules:
  0.0 1008.7 jit_solution(15240779064843754211)
XLA Ops:
  14.8 7.3 all-to-all-start.1
  33.5 7.1 all-to-all-done
  52.0 7.1 fusion.30
  59.1 11.1 %dynamic-slice_bitcast_fusion = (f32[1,8,2,64,512]{4,3,2,1,0:T(8,128)S(1)}, f32[1,8,2,64,512]{4,3,2,1,0:T(8,128)}, f32[1,8,2,64,512]{4,3,2,1,0:T(8,128)}, f32[1,...) fusion(f32[8,2,8,64,512]{4,3,2,1,0:T(8,128)} %bitcast.127, ...), kind=kLoop, calls=%fused_computation.45 | loop fusion | bytes 29360156 | tf_op jit(solution)/shard_map/jit(dynamic_index_in_dim)/dynamic_slice | solution.py:126
  73.6 45.1 %collective-permute-done = f32[1,8,2,64,512]{4,3,2,1,0:T(8,128)S(1)} collective-permute-done((f32[1,8,2,64,512]{4,3,2,1,0:T(8,128)}, f32[1,8,2,64,512]{4,3,2,1,0:T(8,128)S(1)}, u32[]{:S(2)}, u32[]{:S(2)}) %collective-permute-start) | collective-permute-done | bytes 2097184 | tf_op jit(solution)/shard_map/ppermute | solution.py:127
  121.3 43.1 %collective-permute-start.6 = (f32[1,8,2,64,512]{4,3,2,1,0:T(8,128)S(1)}, f32[1,8,2,64,512]{4,3,2,1,0:T(8,128)}, u32[]{:S(2)}, u32[]{:S(2)}) collective-permute-start(f32[1,8,2,64,512]{4,3,2,1,0:T(8,128)S(1)} %get-tuple-element.34), channel_id=1, source_target_pairs={{0,7},{1,0},{2,1},{3,2},{4,3},{5,4},{6,5},{7,6},{8,15},{9,8},{10,9... | collective-permute-start | bytes 6291464 | tf_op jit(solution)/shard_map/ppermute | solution.py:127
  175.5 12.0 %copy.124 = f32[8,2,8,64,512]{4,3,1,0,2:T(8,128)} copy(f32[8,2,8,64,512]{4,3,2,1,0:T(8,128)} %bitcast.128) | data formatting | bytes 33554432 | tf_op jit(solution)/shard_map/reshape | solution.py:17
  195.9 14.3 %collective-permute-done.2 = f32[1,8,2,64,512]{4,3,2,1,0:T(8,128)} collective-permute-done((f32[1,8,2,64,512]{4,3,2,1,0:T(8,128)}, f32[1,8,2,64,512]{4,3,2,1,0:T(8,128)}, u32[]{:S(2)}, u32[]{:S(2)}) %collective-permute-start.2) | collective-permute-done | bytes 2097184 | tf_op jit(solution)/shard_map/ppermute | solution.py:127
  216.5 36.9 %collective-permute-done.4 = f32[1,8,2,64,512]{4,3,2,1,0:T(8,128)} collective-permute-done((f32[1,8,2,64,512]{4,3,2,1,0:T(8,128)}, f32[1,8,2,64,512]{4,3,2,1,0:T(8,128)}, u32[]{:S(2)}, u32[]{:S(2)}) %collective-permute-start.4) | collective-permute-done | bytes 2097184 | tf_op jit(solution)/shard_map/ppermute | solution.py:127
  262.9 33.1 %fusion.11 = f32[2,16,4,64,512]{4,1,3,2,0:T(8,128)} fusion(f32[16,4,2,64,512]{4,3,2,1,0:T(8,128)} %bitcast.130, f32[1,2,16,16]{3,2,1,0:T(8,128)S(1)} %get-tuple-element.51, f32[1,2,16,16]{3,2,1,0:T(8,128)S(1)} %get-tuple-element.50), kind=kOutput, calls=%fused_computation.23 | convolution fusion | flops 1610613760 | bytes 33558528 | tf_op jit(solution)/shard_map/acnt,tvcji->anvji/dot_general | solution.py:138
  296.0 7.1 multiply_subtract_fusion.1
  303.2 6.6 pad_maximum_fusion
  309.7 67.0 %fusion.14 = f32[2,512,16,4,64]{1,4,3,2,0:T(8,128)} fusion(f32[2,16,4,64,512]{4,1,3,2,0:T(8,128)} %pad_maximum_fusion, f32[1,2,512,512]{3,2,1,0:T(8,128)S(1)} %copy-done.1, f32[1,2,512,512]{3,2,1,0:T(8,128)S(1)} %copy-done), kind=kOutput, calls=%fused_computation.24 | convolution fusion | flops 51540656128 | bytes 37748736 | tf_op jit(solution)/shard_map/acmi,cnvji->amnvj/dot_general | solution.py:147
  376.7 31.1 %copy.82 = f32[2,512,16,4,64]{4,3,2,1,0:T(4,128)} copy(f32[2,512,16,4,64]{1,4,3,2,0:T(8,128)} %fusion.14) | data formatting | bytes 33554432 | tf_op jit(solution)/shard_map/acmi,cnvji->amnvj/dot_general | solution.py:147
  407.7 27.2 %reshape.442 = f32[2,1,32,65536]{3,2,0,1:T(8,128)} reshape(f32[2,512,16,4,64]{4,3,2,1,0:T(4,128)} %copy.82) | data formatting | bytes 33554432 | tf_op jit(solution)/shard_map/reshape | solution.py:150
  434.9 28.6 %copy.83 = f32[2,1,32,65536]{3,0,1,2:T(2,128)} copy(f32[2,1,32,65536]{3,2,0,1:T(8,128)} %reshape.442) | data formatting | bytes 33554432 | tf_op jit(solution)/shard_map/reshape | solution.py:150
  463.5 5.8 all-to-all-start.2
  479.0 362.1 %all-to-all-done.2 = f32[2,1,32,65536]{3,0,1,2:T(2,128)} async-done(((f32[2,1,32,65536]{3,0,1,2:T(2,128)}), f32[2,1,32,65536]{3,0,1,2:T(2,128)}, u32[]{:S(2)}, u32[]{:S(2)}) %all-to-all-start.2) | async-done | bytes 16777248 | tf_op jit(solution)/shard_map/all_to_all | solution.py:151
  841.1 38.4 %reshape.494 = f32[2,4,8,256,4,64]{5,4,3,0,2,1:T(4,128)} reshape(f32[2,1,32,65536]{3,0,1,2:T(2,128)} %all-to-all-done.2) | data formatting | bytes 33554432 | tf_op jit(solution)/shard_map/reshape | solution.py:152
  879.5 30.9 %copy.85 = f32[2,4,8,256,4,64]{3,4,1,0,5,2:T(4,128)} copy(f32[2,4,8,256,4,64]{5,4,3,0,2,1:T(4,128)} %reshape.494) | data formatting | bytes 33554432 | tf_op jit(solution)/shard_map/reshape | solution.py:152
  910.4 32.1 %fusion.17 = f32[2,16,8,256,64]{3,1,4,2,0:T(8,128)S(1)} fusion(f32[2,4,8,256,4,64]{3,4,1,0,5,2:T(4,128)} %copy.85, f32[2,2,16,4,4,1,1]{2,4,3,1,6,5,0:T(4,128)S(1)} %maximum_bitcast_fusion.17), kind=kOutput, calls=%fused_computation.25 | convolution fusion | flops 1610612736 | bytes 33558528 | tf_op jit(solution)/shard_map/acnpv,cptrvj->antrj/dot_general | solution.py:154
  947.1 42.3 %fusion.10 = f32[256,512,16]{1,0,2:T(8,128)} fusion(f32[2,16,8,256,64]{3,1,4,2,0:T(8,128)S(1)} %pad_maximum_fusion.1, f32[1,512,8,64]{1,3,2,0:T(8,128)S(1)} %get-tuple-element.63, f32[1,512,8,64]{1,3,2,0:T(8,128)S(1)} %get-tuple-element.64), kind=kOutput, calls=%fused_computation.18 | convolution fusion | flops 25772425216 | bytes 27262976 | tf_op jit(solution)/shard_map/cmtj,cntrj->rmn/dot_general | solution.py:164
  989.4 10.3 %copy.87 = f32[256,512,16]{0,2,1:T(8,128)} copy(f32[256,512,16]{1,0,2:T(8,128)} %fusion.10) | data formatting | bytes 16777216 | tf_op jit(solution)/shard_map/div | solution.py:165
  999.6 8.9 copy.91
  (91 shorter events, 92.0 us)
Async XLA Ops:
  14.8 15.5 %all-to-all-start.1 = ((s32[2,8,32,4]{1,3,0,2:T(4,128)}), s32[2,8,32,4]{1,3,0,2:T(4,128)S(1)}, u32[]{:S(2)}, u32[]{:S(2)}) async-start(s32[2,8,32,4]{1,3,0,2:T(4,128)} %copy.70), calls=%async_computation.1 | async-start | bytes 262144 | tf_op jit(solution)/shard_map/all_to_all | solution.py:80
  30.3 10.3 %all-to-all-start = ((f32[32,1,160]{2,1,0:T(1,128)}), f32[32,1,160]{2,1,0:T(1,128)S(1)}, u32[]{:S(2)}, u32[]{:S(2)}) async-start(f32[32,1,160]{2,1,0:T(1,128)} %reshape.502), calls=%async_computation | async-start | bytes 65536 | tf_op jit(solution)/shard_map/all_to_all | solution.py:73
  70.2 48.5 %collective-permute-start = (f32[1,8,2,64,512]{4,3,2,1,0:T(8,128)}, f32[1,8,2,64,512]{4,3,2,1,0:T(8,128)S(1)}, u32[]{:S(2)}, u32[]{:S(2)}) collective-permute-start(f32[1,8,2,64,512]{4,3,2,1,0:T(8,128)} %get-tuple-element.40), channel_id=1, source_target_pairs={{0,1},{1,2},{2,3},{3,4},{4,5},{5,6},{6,7},{7,0},{8,9},{9,10},{10,1... | collective-permute-start | bytes 6291464 | tf_op jit(solution)/shard_map/ppermute | solution.py:127
  70.3 49.7 %collective-permute-start.1 = (f32[1,8,2,64,512]{4,3,2,1,0:T(8,128)}, f32[1,8,2,64,512]{4,3,2,1,0:T(8,128)S(1)}, u32[]{:S(2)}, u32[]{:S(2)}) collective-permute-start(f32[1,8,2,64,512]{4,3,2,1,0:T(8,128)} %get-tuple-element.39), channel_id=1, source_target_pairs={{0,2},{1,3},{2,4},{3,5},{4,6},{5,7},{6,0},{7,1},{8,10},{9,11},{10,... | collective-permute-start | bytes 6291464 | tf_op jit(solution)/shard_map/ppermute | solution.py:127
  70.8 139.4 %collective-permute-start.2 = (f32[1,8,2,64,512]{4,3,2,1,0:T(8,128)}, f32[1,8,2,64,512]{4,3,2,1,0:T(8,128)}, u32[]{:S(2)}, u32[]{:S(2)}) collective-permute-start(f32[1,8,2,64,512]{4,3,2,1,0:T(8,128)} %get-tuple-element.38), channel_id=1, source_target_pairs={{0,3},{1,4},{2,5},{3,6},{4,7},{5,0},{6,1},{7,2},{8,11},{9,12},{10,... | collective-permute-start | bytes 6291464 | tf_op jit(solution)/shard_map/ppermute | solution.py:127
  72.3 141.0 %collective-permute-start.3 = (f32[1,8,2,64,512]{4,3,2,1,0:T(8,128)}, f32[1,8,2,64,512]{4,3,2,1,0:T(8,128)}, u32[]{:S(2)}, u32[]{:S(2)}) collective-permute-start(f32[1,8,2,64,512]{4,3,2,1,0:T(8,128)} %get-tuple-element.37), channel_id=1, source_target_pairs={{0,4},{1,5},{2,6},{3,7},{4,0},{5,1},{6,2},{7,3},{8,12},{9,13},{10,... | collective-permute-start | bytes 6291464 | tf_op jit(solution)/shard_map/ppermute | solution.py:127
  73.6 179.8 %collective-permute-start.4 = (f32[1,8,2,64,512]{4,3,2,1,0:T(8,128)}, f32[1,8,2,64,512]{4,3,2,1,0:T(8,128)}, u32[]{:S(2)}, u32[]{:S(2)}) collective-permute-start(f32[1,8,2,64,512]{4,3,2,1,0:T(8,128)} %get-tuple-element.36), channel_id=1, source_target_pairs={{0,5},{1,6},{2,7},{3,0},{4,1},{5,2},{6,3},{7,4},{8,13},{9,14},{10,... | collective-permute-start | bytes 6291464 | tf_op jit(solution)/shard_map/ppermute | solution.py:127
  118.7 1.3 copy-start.2
  118.7 137.9 %collective-permute-start.5 = (f32[1,8,2,64,512]{4,3,2,1,0:T(8,128)}, f32[1,8,2,64,512]{4,3,2,1,0:T(8,128)}, u32[]{:S(2)}, u32[]{:S(2)}) collective-permute-start(f32[1,8,2,64,512]{4,3,2,1,0:T(8,128)} %get-tuple-element.35), channel_id=1, source_target_pairs={{0,6},{1,7},{2,0},{3,1},{4,2},{5,3},{6,4},{7,5},{8,14},{9,15},{10,... | collective-permute-start | bytes 6291464 | tf_op jit(solution)/shard_map/ppermute | solution.py:127
  120.0 1.3 copy-start.3
  121.3 138.4 %collective-permute-start.6 = (f32[1,8,2,64,512]{4,3,2,1,0:T(8,128)S(1)}, f32[1,8,2,64,512]{4,3,2,1,0:T(8,128)}, u32[]{:S(2)}, u32[]{:S(2)}) collective-permute-start(f32[1,8,2,64,512]{4,3,2,1,0:T(8,128)S(1)} %get-tuple-element.34), channel_id=1, source_target_pairs={{0,7},{1,0},{2,1},{3,2},{4,3},{5,4},{6,5},{7,6},{8,15},{9,8},{10,9... | collective-permute-start | bytes 6291464 | tf_op jit(solution)/shard_map/ppermute | solution.py:127
  188.3 275.2 %all-to-all-start.3 = ((f32[2,8,32,4]{1,3,0,2:T(4,128)}), f32[2,8,32,4]{1,3,0,2:T(4,128)S(1)}, u32[]{:S(2)}, u32[]{:S(2)}) async-start(f32[2,8,32,4]{1,3,0,2:T(4,128)} %copy.89), calls=%async_computation.3 | async-start | bytes 262144 | tf_op jit(solution)/shard_map/all_to_all | solution.py:113
  191.0 3.3 copy-start.4
  303.1 6.6 copy-start
  303.1 6.6 copy-start.1
  463.5 377.5 %all-to-all-start.2 = ((f32[2,1,32,65536]{3,0,1,2:T(2,128)}), f32[2,1,32,65536]{3,0,1,2:T(2,128)}, u32[]{:S(2)}, u32[]{:S(2)}) async-start(f32[2,1,32,65536]{3,0,1,2:T(2,128)} %copy.83), calls=%async_computation.2 | async-start | bytes 33554432 | tf_op jit(solution)/shard_map/all_to_all | solution.py:151
